TPU v7x, 128 devices: a whole 4x4x4 slice. The times are simulated.
128 devices in a mesh: dp: 4 (over x), expert: 32 (over z, y, core).
Axes of the slice: x: 4, y: 4, z: 4, core: 2. Of those that a mesh axis runs over, the one named last changes fastest.
Arguments:
- tokens: bfloat16 [16384, 7168], P('expert', 'dp'), may hold values from -6 to 6
- grad_out: bfloat16 [16384, 7168], P('expert', 'dp'), may hold values from -6 to 6
- route_ids: int32 [16384, 1], P('expert'), may hold values from 0 to 31; in each aligned block of 512 rows (0 to 511, 512 to 1023, ...) at most 20 rows name the same one
- gate_codes: int32 [16384, 1], P('expert'), may hold values from 1 to 255
- gate_weight: bfloat16 [32, 7168, 1024], P('expert', 'dp'), may hold values from -0.0625 to 0.0625
- up_weight: bfloat16 [32, 7168, 1024], P('expert', 'dp'), may hold values from -0.0625 to 0.0625
- down_weight: bfloat16 [32, 1024, 7168], P('expert', None, 'dp'), may hold values from -0.1875 to 0.1875
- momentum: bfloat16 [32, 1024, 7168], P('expert', None, 'dp'), may hold values from -6 to 6
Outputs:
- grad_tokens: bfloat16 [16384, 7168], P('expert', 'dp')
- new_down: bfloat16 [32, 1024, 7168], P('expert', None, 'dp')
- new_momentum: bfloat16 [32, 1024, 7168], P('expert', None, 'dp')
Inputs may be any that keep to these rules, and one draw needn't show every extreme that they name: `route_ids`: each token names one expert. Among the 512 tokens of one index of the expert axis no expert is named by more than 20 tokens, a bound that some block reaches.
All inputs are finite; a program needn't handle non-finite values.
Results may differ from a plain program's by a relative error of at most 0.022.
Values may be sent and summed in bfloat16 or wider, within the bound.
A program may use at most 128 MiB of HBM per device.

v0:
```python
import jax
import jax.numpy as jnp
from jax import lax
from jax.sharding import PartitionSpec as P

first_beta = 0.9
second_beta = 0.9
learn_rate = 0.01
decay_rate = 3.0
soft_width = 1.0


def activate(terms):
    pre_gate = terms[:, 0, :]
    pre_up = terms[:, 1, :]
    grad_hidden = terms[:, 2, :]
    sigmoid = jax.nn.sigmoid(pre_gate)
    active = pre_gate * sigmoid
    hidden = (active * pre_up).astype(jnp.bfloat16)
    d_gate = (grad_hidden * pre_up * sigmoid * (1.0 + pre_gate * (1.0 - sigmoid))).astype(
        jnp.bfloat16
    )
    d_up = (grad_hidden * active).astype(jnp.bfloat16)
    return (hidden, d_gate, d_up)


def contract_last(left, right):
    return lax.dot_general(
        left, right, (((1,), (1,)), ((), ())), preferred_element_type=jnp.float32
    )


def contract_first(left, right):
    return lax.dot_general(
        left, right, (((0,), (0,)), ((), ())), preferred_element_type=jnp.float32
    )


def local(tokens, grad_out, route_ids, gate_codes, gate_weight, up_weight, down_weight, momentum):
    n_expert = lax.axis_size("expert")
    tok_rows, slab = tokens.shape
    top = route_ids.shape[1]
    capacity = max(2, tok_rows * top * 5 // (4 * n_expert))
    flat_ids = route_ids.reshape(-1)
    expert_iota = jnp.arange(n_expert, dtype=jnp.int32)
    onehot = (flat_ids[:, None] == expert_iota[None, :]).astype(jnp.int32)
    before = jnp.cumsum(onehot, axis=0) - onehot
    slot = jnp.sum(before * onehot, axis=1)
    target = flat_ids * capacity + slot
    slot_iota = jnp.arange(n_expert * capacity, dtype=jnp.int32)
    placed = (
        (target[None, :] == slot_iota[:, None])
        .astype(jnp.float32)
        .reshape(n_expert * capacity, tok_rows, top)
    )
    route_scale = gate_codes.astype(jnp.float32) / 256.0
    picker = jnp.sum(placed, axis=2).astype(jnp.bfloat16)
    scaler = jnp.sum(placed * route_scale[None, :, :], axis=2).astype(jnp.bfloat16)
    send_x = jnp.dot(picker, tokens, preferred_element_type=jnp.float32).astype(jnp.bfloat16)
    send_dy = jnp.dot(scaler, grad_out, preferred_element_type=jnp.float32).astype(jnp.bfloat16)
    send_x = send_x.reshape(n_expert, capacity, slab)
    send_dy = send_dy.reshape(n_expert, capacity, slab)
    recv_x, recv_dy = (
        lax.all_to_all(send_x, "expert", split_axis=0, concat_axis=0, tiled=True),
        lax.all_to_all(send_dy, "expert", split_axis=0, concat_axis=0, tiled=True),
    )
    x_rows = recv_x.reshape(-1, slab)
    dy_rows = recv_dy.reshape(-1, slab)
    w_gate = gate_weight[0]
    w_up = up_weight[0]
    w_down = down_weight[0]
    dy_part = dy_rows
    gate_part = jnp.dot(x_rows, w_gate, preferred_element_type=jnp.float32)
    up_part = jnp.dot(x_rows, w_up, preferred_element_type=jnp.float32)
    back_part = contract_last(dy_part, w_down)
    shares = lax.psum_scatter(
        jnp.stack([gate_part, up_part, back_part], axis=1).astype(jnp.bfloat16),
        "dp",
        scatter_dimension=0,
        tiled=True,
    ).astype(jnp.float32)
    hidden, d_gate, d_up = activate(shares)
    hidden_part = lax.all_gather(hidden, "dp", axis=0, tiled=True)
    gate_part = lax.all_gather(d_gate, "dp", axis=0, tiled=True)
    up_part = lax.all_gather(d_up, "dp", axis=0, tiled=True)
    dy_part = dy_rows
    grad_w = contract_first(hidden_part, dy_part)
    rows_x = contract_last(gate_part, w_gate) + contract_last(up_part, w_up)
    grad_x = rows_x
    grad_down, grad_x = (grad_w, grad_x)
    back = grad_x.astype(jnp.bfloat16).reshape(n_expert, capacity, slab)
    returned = lax.all_to_all(back, "expert", split_axis=0, concat_axis=0, tiled=True)
    returned = returned.reshape(n_expert * capacity, slab)
    grad_tokens = contract_first(picker, returned).astype(jnp.bfloat16)
    moment = momentum[0].astype(jnp.float32)
    weight = w_down.astype(jnp.float32)
    blend = first_beta * moment + (1.0 - first_beta) * grad_down
    step = blend / jnp.sqrt(blend * blend + soft_width * soft_width)
    agree = jnp.maximum(step * jnp.sign(weight), 0.0)
    new_down = (weight - learn_rate * (step + decay_rate * agree * weight)).astype(jnp.bfloat16)
    new_moment = (second_beta * moment + (1.0 - second_beta) * grad_down).astype(jnp.bfloat16)
    return (grad_tokens, new_down[None], new_moment[None])


def solution(mesh):
    placed = (
        P("expert", "dp"),
        P("expert", "dp"),
        P("expert", None),
        P("expert", None),
        P("expert", "dp", None),
        P("expert", "dp", None),
        P("expert", None, "dp"),
        P("expert", None, "dp"),
    )
    return jax.shard_map(
        local,
        mesh=mesh,
        in_specs=placed,
        out_specs=(P("expert", "dp"), P("expert", None, "dp"), P("expert", None, "dp")),
        check_vma=False,
    )
```

profile of v0, /device:TPU:0, one launch (start us, length us, event | category | flops | bytes accessed | tf_op | source)
XLA Modules:
  0.0 284.5 jit_solution(3125101756731378622)
XLA Ops:
  7.2 0.0 copy-start
  7.2 0.8 fusion.48
  8.0 1.2 reduce-window.6
  9.2 0.2 slice_reduce_fusion
  9.4 0.8 fusion.47
  10.2 0.7 multiply_add_fusion
  10.9 0.0 copy-done
  10.9 2.7 convolution_convert_fusion.1
  13.6 4.1 %reshape.132 = bf16[32,20,1792]{2,1,0:T(8,128)(2,1)} reshape(bf16[640,1792]{1,0:T(8,128)(2,1)} %convolution_convert_fusion.1) | data formatting | bytes 4587520 | tf_op jit(solution)/shard_map/reshape | solution.py:61
  17.7 0.0 copy-start.5
  17.7 8.5 %all-to-all-start = ((bf16[32,20,1792]{2,1,0:T(8,128)(2,1)}), bf16[32,20,1792]{2,1,0:T(8,128)(2,1)S(1)}, u32[]{:S(2)}, u32[]{:S(2)}) async-start(bf16[32,20,1792]{2,1,0:T(8,128)(2,1)} %reshape.132), calls=%async_computation | async-start | bytes 5505024 | tf_op jit(solution)/shard_map/all_to_all | solution.py:64
  26.3 0.0 copy-done.5
  26.3 4.3 %convolution_convert_fusion = bf16[640,1792]{1,0:T(8,128)(2,1)} fusion(bf16[512,1792]{1,0:T(8,128)(2,1)} %param.9, f32[512]{0:T(512)S(1)} %bitcast.104, s32[512]{0:T(512)S(1)} %multiply_add_fusion), kind=kOutput, calls=%fused_computation.24 | convolution fusion | flops 1176207360 | bytes 4132864 | tf_op jit(solution)/shard_map/dot_general | solution.py:60
  30.6 4.1 %reshape.134 = bf16[32,20,1792]{2,1,0:T(8,128)(2,1)} reshape(bf16[640,1792]{1,0:T(8,128)(2,1)} %convolution_convert_fusion) | data formatting | bytes 4587520 | tf_op jit(solution)/shard_map/reshape | solution.py:62
  34.7 29.1 %all-to-all-done = bf16[32,20,1792]{2,1,0:T(8,128)(2,1)S(1)} async-done(((bf16[32,20,1792]{2,1,0:T(8,128)(2,1)}), bf16[32,20,1792]{2,1,0:T(8,128)(2,1)S(1)}, u32[]{:S(2)}, u32[]{:S(2)}) %all-to-all-start) | async-done | bytes 2293792 | tf_op jit(solution)/shard_map/all_to_all | solution.py:64
  63.8 4.8 %all-to-all-start.1 = ((bf16[32,20,1792]{2,1,0:T(8,128)(2,1)}), bf16[32,20,1792]{2,1,0:T(8,128)(2,1)}, u32[]{:S(2)}, u32[]{:S(2)}) async-start(bf16[32,20,1792]{2,1,0:T(8,128)(2,1)} %reshape.134), calls=%async_computation.1 | async-start | bytes 5505024 | tf_op jit(solution)/shard_map/all_to_all | solution.py:65
  68.6 0.0 reduce-scatter.2.cloned.1.call-start
  68.6 2.1 reshape.133
  70.7 0.0 copy-start.2
  70.7 0.0 copy-start.6
  70.7 6.5 %fusion.31 = bf16[640,1,1024]{2,0,1:T(8,128)(2,1)} fusion(bf16[640,1792]{1,0:T(8,128)(2,1)} %reshape.133, bf16[1,1792,1024]{2,1,0:T(8,128)(2,1)} %param.13), kind=kOutput, calls=%fused_computation.31 | convolution fusion | flops 2349465600 | bytes 7274496 | tf_op jit(solution)/shard_map/dot_general | solution.py:74
  77.2 0.0 copy-done.2
  77.2 0.0 copy-done.6
  77.2 3.6 %fusion.34 = bf16[640,1,1024]{2,0,1:T(8,128)(2,1)} fusion(bf16[640,1792]{1,0:T(8,128)(2,1)S(1)} %copy-done.2, bf16[1,1792,1024]{2,1,0:T(8,128)(2,1)S(1)} %copy-done.6), kind=kOutput, calls=%fused_computation.32 | convolution fusion | flops 2349465600 | bytes 7274496 | tf_op jit(solution)/shard_map/dot_general | solution.py:73
  80.8 25.3 %all-to-all-done.1 = bf16[32,20,1792]{2,1,0:T(8,128)(2,1)} async-done(((bf16[32,20,1792]{2,1,0:T(8,128)(2,1)}), bf16[32,20,1792]{2,1,0:T(8,128)(2,1)}, u32[]{:S(2)}, u32[]{:S(2)}) %all-to-all-start.1) | async-done | bytes 2293792 | tf_op jit(solution)/shard_map/all_to_all | solution.py:65
  106.1 2.7 reshape.135
  108.8 0.0 copy-start.3
  108.8 0.0 copy-start.4
  108.8 4.8 %fusion.28 = bf16[640,1,1024]{2,0,1:T(8,128)(2,1)S(1)} fusion(bf16[640,1792]{1,0:T(8,128)(2,1)S(1)} %reshape.135, bf16[1,1024,1792]{2,1,0:T(8,128)(2,1)} %param.14), kind=kOutput, calls=%fused_computation.30 | convolution fusion | flops 2349465600 | bytes 7274496 | tf_op jit(solution)/shard_map/dot_general | solution.py:28
  113.6 0.0 copy-done.3
  113.6 0.0 copy-done.4
  113.6 2.1 pad_maximum_fusion
  115.7 0.0 reduce-scatter.2.cloned.1.call-update
  115.7 0.0 all-gather.6.cloned.1.call-start
  115.8 41.3 %reduce-scatter.2.cloned.1.call-done = bf16[160,3,1024]{2,0,1:T(8,128)(2,1)} async-done(((bf16[640,3,1024]{2,0,1:T(8,128)(2,1)}), bf16[160,3,1024]{2,0,1:T(8,128)(2,1)}) %reduce-scatter.2.cloned.1.call-update) | async-done | bytes 983056 | tf_op jit(solution)/shard_map/reduce_scatter | solution.py:76
  157.1 1.4 convert_element_type.104
  158.5 1.4 multiply_convert_fusion
  159.9 0.0 all-gather.6.cloned.1.call-update
  159.9 0.0 all-gather.4.cloned.1.call-start
  159.9 0.7 all-gather.4.cloned.1.call-update
  160.6 0.2 all-gather.8.cloned.1.call-start
  160.8 0.3 all-gather.8.cloned.1.call-update
  161.2 23.5 %all-gather.6.cloned.1.call-done = bf16[640,1024]{1,0:T(8,128)(2,1)} async-done(((bf16[160,1024]{1,0:T(8,128)(2,1)}), bf16[640,1024]{1,0:T(8,128)(2,1)}) %all-gather.6.cloned.1.call-update) | async-done | bytes 1310736 | tf_op jit(solution)/shard_map/all_gather | solution.py:85
  184.7 7.1 %fusion.8 = f32[640,1792]{1,0:T(8,128)} fusion(bf16[640,1024]{1,0:T(8,128)(2,1)} %all-gather.6.cloned.1.call-done, bf16[1,1792,1024]{2,1,0:T(8,128)(2,1)} %param.13), kind=kOutput, calls=%fused_computation.14 | convolution fusion | flops 2348810240 | bytes 9568256 | tf_op jit(solution)/shard_map/dot_general | solution.py:28
  191.8 20.6 %all-gather.4.cloned.1.call-done = bf16[640,1024]{1,0:T(8,128)(2,1)} async-done(((bf16[160,1024]{1,0:T(8,128)(2,1)}), bf16[640,1024]{1,0:T(8,128)(2,1)}) %all-gather.4.cloned.1.call-update) | async-done | bytes 1310736 | tf_op jit(solution)/shard_map/all_gather | solution.py:84
  212.4 7.8 %add_convert_fusion = bf16[640,1792]{1,0:T(8,128)(2,1)} fusion(f32[640,1792]{1,0:T(8,128)} %fusion.8, bf16[640,1024]{1,0:T(8,128)(2,1)} %all-gather.4.cloned.1.call-done, bf16[1,1792,1024]{2,1,0:T(8,128)(2,1)} %param.12), kind=kOutput, calls=%fused_computation.10 | convolution fusion | flops 2351104000 | bytes 11862016 | tf_op jit(solution)/shard_map/dot_general | solution.py:28
  220.2 4.1 %reshape.136 = bf16[32,20,1792]{2,1,0:T(8,128)(2,1)} reshape(bf16[640,1792]{1,0:T(8,128)(2,1)} %add_convert_fusion) | data formatting | bytes 4587520 | tf_op jit(solution)/shard_map/reshape | solution.py:91
  224.3 7.4 %all-to-all-start.2 = ((bf16[32,20,1792]{2,1,0:T(8,128)(2,1)}), bf16[32,20,1792]{2,1,0:T(8,128)(2,1)}, u32[]{:S(2)}, u32[]{:S(2)}) async-start(bf16[32,20,1792]{2,1,0:T(8,128)(2,1)} %reshape.136), calls=%async_computation.3 | async-start | bytes 5505024 | tf_op jit(solution)/shard_map/all_to_all | solution.py:92
  231.7 8.3 %all-gather.8.cloned.1.call-done = bf16[640,1024]{1,0:T(8,128)(2,1)} async-done(((bf16[160,1024]{1,0:T(8,128)(2,1)}), bf16[640,1024]{1,0:T(8,128)(2,1)}) %all-gather.8.cloned.1.call-update) | async-done | bytes 1310736 | tf_op jit(solution)/shard_map/all_gather | solution.py:83
  240.0 12.7 %convert_bitcast_fusion = (bf16[1,1024,1792]{2,1,0:T(8,128)(2,1)}, bf16[1,1024,1792]{2,1,0:T(8,128)(2,1)}) fusion(bf16[1,1024,1792]{2,1,0:T(8,128)(2,1)} %param.14, bf16[640,1024]{1,0:T(8,128)(2,1)} %all-gather.8.cloned.1.call-done, bf16[640,1792]{1,0:T(8,128)(2,1)S(1)} %reshape.135, bf16[1,1024,1792]{2,1,0:T(8,128)(2,1)} %param.15), kind=kOutput, calls=%fused_computation.22 | convolution fusion | flops 2381840384 | bytes 18284544 | tf_op jit(solution)/shard_map/dot_general | solution.py:34
  252.7 16.5 %all-to-all-done.2 = bf16[32,20,1792]{2,1,0:T(8,128)(2,1)} async-done(((bf16[32,20,1792]{2,1,0:T(8,128)(2,1)}), bf16[32,20,1792]{2,1,0:T(8,128)(2,1)}, u32[]{:S(2)}, u32[]{:S(2)}) %all-to-all-start.2) | async-done | bytes 2293792 | tf_op jit(solution)/shard_map/all_to_all | solution.py:92
  269.1 0.0 copy-start.1
  269.1 4.3 %reshape.137 = bf16[640,1792]{1,0:T(8,128)(2,1)} reshape(bf16[32,20,1792]{2,1,0:T(8,128)(2,1)} %all-to-all-done.2) | data formatting | bytes 4587520 | tf_op jit(solution)/shard_map/reshape | solution.py:93
  273.4 4.5 %convolution_convert_fusion.2 = bf16[512,1792]{1,0:T(8,128)(2,1)} fusion(bf16[640,1792]{1,0:T(8,128)(2,1)} %reshape.137, s32[512]{0:T(512)S(1)} %multiply_add_fusion), kind=kOutput, calls=%fused_computation.26 | convolution fusion | flops 1176305664 | bytes 4130816 | tf_op jit(solution)/shard_map/dot_general | solution.py:34
  277.9 0.0 copy-done.1
  (3 shorter events, 0.0 us)
Async XLA Ops:
  7.2 3.7 %copy-start = (bf16[512,1792]{1,0:T(8,128)(2,1)S(1)}, bf16[512,1792]{1,0:T(8,128)(2,1)}, u32[]{:S(2)}) copy-start(bf16[512,1792]{1,0:T(8,128)(2,1)} %param.8) | copy-start | bytes 5505028
  17.7 8.6 %copy-start.5 = (s32[512,1]{0,1:T(1,128)S(1)}, s32[512,1]{0,1:T(1,128)}, u32[]{:S(2)}) copy-start(s32[512,1]{0,1:T(1,128)} %param.11) | copy-start | bytes 6148
  17.7 46.0 %all-to-all-start = ((bf16[32,20,1792]{2,1,0:T(8,128)(2,1)}), bf16[32,20,1792]{2,1,0:T(8,128)(2,1)S(1)}, u32[]{:S(2)}, u32[]{:S(2)}) async-start(bf16[32,20,1792]{2,1,0:T(8,128)(2,1)} %reshape.132), calls=%async_computation | async-start | bytes 5505024 | tf_op jit(solution)/shard_map/all_to_all | solution.py:64
  63.8 42.3 %all-to-all-start.1 = ((bf16[32,20,1792]{2,1,0:T(8,128)(2,1)}), bf16[32,20,1792]{2,1,0:T(8,128)(2,1)}, u32[]{:S(2)}, u32[]{:S(2)}) async-start(bf16[32,20,1792]{2,1,0:T(8,128)(2,1)} %reshape.134), calls=%async_computation.1 | async-start | bytes 5505024 | tf_op jit(solution)/shard_map/all_to_all | solution.py:65
  68.6 88.5 %reduce-scatter.2.cloned.1.call-start = ((), (), s32[]{:S(2)}) async-start(), calls=%async_computation.4 | async-start | bytes 4915200 | tf_op jit(solution)/shard_map/reduce_scatter | solution.py:76
  70.7 6.5 %copy-start.2 = (bf16[640,1792]{1,0:T(8,128)(2,1)S(1)}, bf16[640,1792]{1,0:T(8,128)(2,1)}, u32[]{:S(2)}) copy-start(bf16[640,1792]{1,0:T(8,128)(2,1)} %reshape.133) | copy-start | bytes 6881284
  70.7 6.5 %copy-start.6 = (bf16[1,1792,1024]{2,1,0:T(8,128)(2,1)S(1)}, bf16[1,1792,1024]{2,1,0:T(8,128)(2,1)}, u32[]{:S(2)}) copy-start(bf16[1,1792,1024]{2,1,0:T(8,128)(2,1)} %param.12) | copy-start | bytes 11010052
  108.8 4.8 %copy-start.3 = (bf16[640,1,1024]{2,0,1:T(8,128)(2,1)S(1)}, bf16[640,1,1024]{2,0,1:T(8,128)(2,1)}, u32[]{:S(2)}) copy-start(bf16[640,1,1024]{2,0,1:T(8,128)(2,1)} %fusion.31) | copy-start | bytes 3932164
  108.8 4.8 %copy-start.4 = (bf16[640,1,1024]{2,0,1:T(8,128)(2,1)S(1)}, bf16[640,1,1024]{2,0,1:T(8,128)(2,1)}, u32[]{:S(2)}) copy-start(bf16[640,1,1024]{2,0,1:T(8,128)(2,1)} %fusion.34) | copy-start | bytes 3932164
  115.7 69.0 %all-gather.6.cloned.1.call-start = ((), (), s32[]{:S(2)}) async-start(), calls=%async_computation.6 | async-start | bytes 1638400 | tf_op jit(solution)/shard_map/all_gather | solution.py:85
  159.9 52.5 %all-gather.4.cloned.1.call-start = ((), (), s32[]{:S(2)}) async-start(), calls=%async_computation.5 | async-start | bytes 1638400 | tf_op jit(solution)/shard_map/all_gather | solution.py:84
  160.6 79.4 %all-gather.8.cloned.1.call-start = ((), (), s32[]{:S(2)}) async-start(), calls=%async_computation.7 | async-start | bytes 1638400 | tf_op jit(solution)/shard_map/all_gather | solution.py:83
  224.3 44.8 %all-to-all-start.2 = ((bf16[32,20,1792]{2,1,0:T(8,128)(2,1)}), bf16[32,20,1792]{2,1,0:T(8,128)(2,1)}, u32[]{:S(2)}, u32[]{:S(2)}) async-start(bf16[32,20,1792]{2,1,0:T(8,128)(2,1)} %reshape.136), calls=%async_computation.3 | async-start | bytes 5505024 | tf_op jit(solution)/shard_map/all_to_all | solution.py:92
  269.1 8.8 %copy-start.1 = (bf16[512,1792]{1,0:T(8,128)(2,1)S(1)}, bf16[512,1792]{1,0:T(8,128)(2,1)}, u32[]{:S(2)}) copy-start(bf16[512,1792]{1,0:T(8,128)(2,1)} %param.8) | copy-start | bytes 5505028
Sparse Core Ops, SparseCore 0:
  115.8 41.1 reduce-scatter.1
  160.0 24.6 all-gather.5
  186.9 25.4 all-gather.3
  214.5 25.4 all-gather.7
where the time goes:
time: 285 us; the launch traced here: 284 us
  waiting for transfers between devices  166 us (58%)
  matrix products  53.9 us (19%)
  local copies, waits for them, and re-layouts  21.6 us (8%)
  starting transfers between devices  21.1 us (7%)
  between operations  13.9 us (5%)
  other arithmetic  8.4 us (3%)
    reduce_scatter x1, waiting for transfers between devices, local(): lax.psum_scatter(jnp.stack([gate_part, up_part, back_part], axis=1).astyp...  41.3 us
    all_to_all x1, waiting for transfers between devices, local(): lax.all_to_all(send_x, 'expert', split_axis=0, concat_axis=0, tiled=True)  29.1 us
    all_to_all x1, waiting for transfers between devices, local(): lax.all_to_all(send_dy, 'expert', split_axis=0, concat_axis=0, tiled=True)  25.3 us
    all_gather x1, waiting for transfers between devices, local(): up_part = lax.all_gather(d_up, 'dp', axis=0, tiled=True)  23.5 us
    all_gather x1, waiting for transfers between devices, local(): gate_part = lax.all_gather(d_gate, 'dp', axis=0, tiled=True)  20.6 us
    dot_general x3, matrix products, contract_last(): lax.dot_general(left, right, (((1,), (1,)), ((), ())), preferred_element_...  19.6 us
    dot_general x2, matrix products, contract_first(): lax.dot_general(left, right, (((0,), (0,)), ((), ())), preferred_element_...  17.2 us
    all_to_all x1, waiting for transfers between devices, local(): lax.all_to_all(back, 'expert', split_axis=0, concat_axis=0, tiled=True)  16.5 us
  transfers between devices with their start and end apart: 7, of which 7 were waited for; matrix products, arithmetic and copies ran while one was open for 18% of the time, Pallas kernels for 0%

commit v1 on v0

--- a/solution.py
+++ b/solution.py
@@ -2,6 +2,7 @@
 import jax.numpy as jnp
 from jax import lax
 from jax.sharding import PartitionSpec as P
+from jax.lax import all_gather
 
 first_beta = 0.9
 second_beta = 0.9
@@ -80,8 +81,17 @@
         tiled=True,
     ).astype(jnp.float32)
     hidden, d_gate, d_up = activate(shares)
-    hidden_part = lax.all_gather(hidden, "dp", axis=0, tiled=True)
-    gate_part = lax.all_gather(d_gate, "dp", axis=0, tiled=True)
+
+    def play_pools(vec, xin, lane_axis):
+        return jnp.split(
+            all_gather(
+                jnp.concatenate([vec, xin], axis=1), axis_name=lane_axis, axis=0, tiled=True
+            ),
+            [vec.shape[1]],
+            axis=1,
+        )
+
+    hidden_part, gate_part = play_pools(hidden, xin=d_gate, lane_axis="dp")
     up_part = lax.all_gather(d_up, "dp", axis=0, tiled=True)
     dy_part = dy_rows
     grad_w = contract_first(hidden_part, dy_part)

time: 285 us -> 295 us (1.035)
  waiting for transfers between devices: 166 us -> 175 us
    all_to_all x1, waiting for transfers between devices: 16.5 us -> 24.8 us  [local(): lax.all_to_all(back, 'expert', split_axis=0, concat_axis=0, tiled=True)]
    all_gather x2 -> x1, waiting for transfers between devices: 29 us -> 30.9 us  [play_pools(): all_gather(jnp.concatenate([vec, xin], axis=1), axis_name=lane_axis, axis...]
  transfers between devices with their start and end apart: 7 -> 6, of which waited for: 7 -> 6; matrix products, arithmetic and copies ran while one was open for 18% -> 14% of each run, Pallas kernels for 0% -> 0%
where the time goes in v1:
time: 295 us
  waiting for transfers between devices  175 us (59%)
  matrix products  53.9 us (18%)
  local copies, waits for them, and re-layouts  21.6 us (7%)
  starting transfers between devices  21 us (7%)
  between operations  13.9 us (5%)
  other arithmetic  9.08 us (3%)
    reduce_scatter x1, waiting for transfers between devices, local(): lax.psum_scatter(jnp.stack([gate_part, up_part, back_part], axis=1).astyp...  41.3 us
    all_gather x1, waiting for transfers between devices, play_pools(): all_gather(jnp.concatenate([vec, xin], axis=1), axis_name=lane_axis, axis...  30.9 us
    all_to_all x1, waiting for transfers between devices, local(): lax.all_to_all(send_x, 'expert', split_axis=0, concat_axis=0, tiled=True)  29.1 us
    all_to_all x1, waiting for transfers between devices, local(): lax.all_to_all(send_dy, 'expert', split_axis=0, concat_axis=0, tiled=True)  25.3 us
    all_to_all x1, waiting for transfers between devices, local(): lax.all_to_all(back, 'expert', split_axis=0, concat_axis=0, tiled=True)  24.8 us
    all_gather x1, waiting for transfers between devices, local(): up_part = lax.all_gather(d_up, 'dp', axis=0, tiled=True)  23.6 us
    dot_general x3, matrix products, contract_last(): lax.dot_general(left, right, (((1,), (1,)), ((), ())), preferred_element_...  19.6 us
    dot_general x2, matrix products, contract_first(): lax.dot_general(left, right, (((0,), (0,)), ((), ())), preferred_element_...  17.2 us
  transfers between devices with their start and end apart: 6, of which 6 were waited for; matrix products, arithmetic and copies ran while one was open for 14% of the time, Pallas kernels for 0%

profile of v1, /device:TPU:0, one launch (start us, length us, event | category | flops | bytes accessed | tf_op | source)
XLA Modules:
  0.0 294.6 jit_solution(3567743396176133277)
XLA Ops:
  7.2 0.0 copy-start
  7.2 0.8 fusion.50
  8.0 1.2 reduce-window.6
  9.2 0.2 slice_reduce_fusion
  9.4 0.8 fusion.49
  10.2 0.7 multiply_add_fusion
  10.9 0.0 copy-done
  10.9 2.7 convolution_convert_fusion.1
  13.6 4.1 %reshape.132 = bf16[32,20,1792]{2,1,0:T(8,128)(2,1)} reshape(bf16[640,1792]{1,0:T(8,128)(2,1)} %convolution_convert_fusion.1) | data formatting | bytes 4587520 | tf_op jit(solution)/shard_map/reshape | solution.py:62
  17.7 0.0 copy-start.5
  17.7 8.5 %all-to-all-start = ((bf16[32,20,1792]{2,1,0:T(8,128)(2,1)}), bf16[32,20,1792]{2,1,0:T(8,128)(2,1)S(1)}, u32[]{:S(2)}, u32[]{:S(2)}) async-start(bf16[32,20,1792]{2,1,0:T(8,128)(2,1)} %reshape.132), calls=%async_computation | async-start | bytes 5505024 | tf_op jit(solution)/shard_map/all_to_all | solution.py:65
  26.3 0.0 copy-done.5
  26.3 4.2 %convolution_convert_fusion = bf16[640,1792]{1,0:T(8,128)(2,1)} fusion(bf16[512,1792]{1,0:T(8,128)(2,1)} %param.9, f32[512]{0:T(512)S(1)} %bitcast.102, s32[512]{0:T(512)S(1)} %multiply_add_fusion), kind=kOutput, calls=%fused_computation.24 | convolution fusion | flops 1176207360 | bytes 4132864 | tf_op jit(solution)/shard_map/dot_general | solution.py:61
  30.6 4.1 %reshape.134 = bf16[32,20,1792]{2,1,0:T(8,128)(2,1)} reshape(bf16[640,1792]{1,0:T(8,128)(2,1)} %convolution_convert_fusion) | data formatting | bytes 4587520 | tf_op jit(solution)/shard_map/reshape | solution.py:63
  34.6 29.1 %all-to-all-done = bf16[32,20,1792]{2,1,0:T(8,128)(2,1)S(1)} async-done(((bf16[32,20,1792]{2,1,0:T(8,128)(2,1)}), bf16[32,20,1792]{2,1,0:T(8,128)(2,1)S(1)}, u32[]{:S(2)}, u32[]{:S(2)}) %all-to-all-start) | async-done | bytes 2293792 | tf_op jit(solution)/shard_map/all_to_all | solution.py:65
  63.8 4.8 %all-to-all-start.1 = ((bf16[32,20,1792]{2,1,0:T(8,128)(2,1)}), bf16[32,20,1792]{2,1,0:T(8,128)(2,1)}, u32[]{:S(2)}, u32[]{:S(2)}) async-start(bf16[32,20,1792]{2,1,0:T(8,128)(2,1)} %reshape.134), calls=%async_computation.1 | async-start | bytes 5505024 | tf_op jit(solution)/shard_map/all_to_all | solution.py:66
  68.6 0.0 reduce-scatter.2.cloned.1.call-start
  68.6 2.1 reshape.133
  70.7 0.0 copy-start.2
  70.7 0.0 copy-start.6
  70.7 6.5 %fusion.31 = bf16[640,1,1024]{2,0,1:T(8,128)(2,1)} fusion(bf16[640,1792]{1,0:T(8,128)(2,1)} %reshape.133, bf16[1,1792,1024]{2,1,0:T(8,128)(2,1)} %param.13), kind=kOutput, calls=%fused_computation.31 | convolution fusion | flops 2349465600 | bytes 7274496 | tf_op jit(solution)/shard_map/dot_general | solution.py:75
  77.2 0.0 copy-done.2
  77.2 0.0 copy-done.6
  77.2 3.6 %fusion.34 = bf16[640,1,1024]{2,0,1:T(8,128)(2,1)} fusion(bf16[640,1792]{1,0:T(8,128)(2,1)S(1)} %copy-done.2, bf16[1,1792,1024]{2,1,0:T(8,128)(2,1)S(1)} %copy-done.6), kind=kOutput, calls=%fused_computation.32 | convolution fusion | flops 2349465600 | bytes 7274496 | tf_op jit(solution)/shard_map/dot_general | solution.py:74
  80.8 25.3 %all-to-all-done.1 = bf16[32,20,1792]{2,1,0:T(8,128)(2,1)} async-done(((bf16[32,20,1792]{2,1,0:T(8,128)(2,1)}), bf16[32,20,1792]{2,1,0:T(8,128)(2,1)}, u32[]{:S(2)}, u32[]{:S(2)}) %all-to-all-start.1) | async-done | bytes 2293792 | tf_op jit(solution)/shard_map/all_to_all | solution.py:66
  106.1 2.7 reshape.135
  108.8 0.0 copy-start.3
  108.8 0.0 copy-start.4
  108.8 4.7 %fusion.28 = bf16[640,1,1024]{2,0,1:T(8,128)(2,1)S(1)} fusion(bf16[640,1792]{1,0:T(8,128)(2,1)S(1)} %reshape.135, bf16[1,1024,1792]{2,1,0:T(8,128)(2,1)} %param.14), kind=kOutput, calls=%fused_computation.30 | convolution fusion | flops 2349465600 | bytes 7274496 | tf_op jit(solution)/shard_map/dot_general | solution.py:29
  113.5 0.0 copy-done.3
  113.6 0.0 copy-done.4
  113.6 2.1 pad_maximum_fusion
  115.7 0.0 reduce-scatter.2.cloned.1.call-update
  115.7 0.0 all-gather.5.cloned.1.call-start
  115.7 41.3 %reduce-scatter.2.cloned.1.call-done = bf16[160,3,1024]{2,0,1:T(8,128)(2,1)} async-done(((bf16[640,3,1024]{2,0,1:T(8,128)(2,1)}), bf16[160,3,1024]{2,0,1:T(8,128)(2,1)}) %reduce-scatter.2.cloned.1.call-update) | async-done | bytes 983056 | tf_op jit(solution)/shard_map/reduce_scatter | solution.py:77
  157.1 1.4 convert_element_type.104
  158.5 1.2 multiply_convert_fusion.2
  159.7 0.0 all-gather.5.cloned.1.call-update
  159.7 0.2 all-gather.3.cloned.1.call-start
  159.9 0.9 pad_maximum_fusion.1
  160.8 0.0 all-gather.3.cloned.1.call-update
  160.8 23.6 %all-gather.5.cloned.1.call-done = bf16[640,1024]{1,0:T(8,128)(2,1)} async-done(((bf16[160,1024]{1,0:T(8,128)(2,1)}), bf16[640,1024]{1,0:T(8,128)(2,1)}) %all-gather.5.cloned.1.call-update) | async-done | bytes 1310736 | tf_op jit(solution)/shard_map/all_gather | solution.py:95
  184.5 7.1 %fusion.8 = f32[640,1792]{1,0:T(8,128)} fusion(bf16[640,1024]{1,0:T(8,128)(2,1)} %all-gather.5.cloned.1.call-done, bf16[1,1792,1024]{2,1,0:T(8,128)(2,1)} %param.13), kind=kOutput, calls=%fused_computation.14 | convolution fusion | flops 2348810240 | bytes 9568256 | tf_op jit(solution)/shard_map/dot_general | solution.py:29
  191.6 30.9 %all-gather.3.cloned.1.call-done = bf16[640,2048]{1,0:T(8,128)(2,1)} async-done(((bf16[160,2048]{1,0:T(8,128)(2,1)}), bf16[640,2048]{1,0:T(8,128)(2,1)}) %all-gather.3.cloned.1.call-update) | async-done | bytes 2621456 | tf_op jit(solution)/shard_map/all_gather | solution.py:87
  222.5 7.8 %add_convert_fusion = bf16[640,1792]{1,0:T(8,128)(2,1)} fusion(f32[640,1792]{1,0:T(8,128)} %fusion.8, bf16[1,1792,1024]{2,1,0:T(8,128)(2,1)} %param.12, bf16[640,2048]{1,0:T(8,128)(2,1)} %all-gather.3.cloned.1.call-done), kind=kOutput, calls=%fused_computation.10 | convolution fusion | flops 2351104000 | bytes 11862016 | tf_op jit(solution)/shard_map/dot_general | solution.py:29
  230.3 4.1 %reshape.136 = bf16[32,20,1792]{2,1,0:T(8,128)(2,1)} reshape(bf16[640,1792]{1,0:T(8,128)(2,1)} %add_convert_fusion) | data formatting | bytes 4587520 | tf_op jit(solution)/shard_map/reshape | solution.py:101
  234.4 7.4 %all-to-all-start.2 = ((bf16[32,20,1792]{2,1,0:T(8,128)(2,1)}), bf16[32,20,1792]{2,1,0:T(8,128)(2,1)}, u32[]{:S(2)}, u32[]{:S(2)}) async-start(bf16[32,20,1792]{2,1,0:T(8,128)(2,1)} %reshape.136), calls=%async_computation.3 | async-start | bytes 5505024 | tf_op jit(solution)/shard_map/all_to_all | solution.py:102
  241.8 12.7 %convert_bitcast_fusion = (bf16[1,1024,1792]{2,1,0:T(8,128)(2,1)}, bf16[1,1024,1792]{2,1,0:T(8,128)(2,1)}) fusion(bf16[1,1024,1792]{2,1,0:T(8,128)(2,1)} %param.14, bf16[640,1792]{1,0:T(8,128)(2,1)S(1)} %reshape.135, bf16[640,2048]{1,0:T(8,128)(2,1)} %all-gather.3.cloned.1.call-done, bf16[1,1024,1792]{2,1,0:T(8,128)(2,1)} %param.15), kind=kOutput, calls=%fused_computation.22 | convolution fusion | flops 2381840384 | bytes 18284544 | tf_op jit(solution)/shard_map/dot_general | solution.py:35
  254.5 24.8 %all-to-all-done.2 = bf16[32,20,1792]{2,1,0:T(8,128)(2,1)} async-done(((bf16[32,20,1792]{2,1,0:T(8,128)(2,1)}), bf16[32,20,1792]{2,1,0:T(8,128)(2,1)}, u32[]{:S(2)}, u32[]{:S(2)}) %all-to-all-start.2) | async-done | bytes 2293792 | tf_op jit(solution)/shard_map/all_to_all | solution.py:102
  279.3 0.0 copy-start.1
  279.3 4.3 %reshape.137 = bf16[640,1792]{1,0:T(8,128)(2,1)} reshape(bf16[32,20,1792]{2,1,0:T(8,128)(2,1)} %all-to-all-done.2) | data formatting | bytes 4587520 | tf_op jit(solution)/shard_map/reshape | solution.py:103
  283.5 4.5 %convolution_convert_fusion.2 = bf16[512,1792]{1,0:T(8,128)(2,1)} fusion(bf16[640,1792]{1,0:T(8,128)(2,1)} %reshape.137, s32[512]{0:T(512)S(1)} %multiply_add_fusion), kind=kOutput, calls=%fused_computation.26 | convolution fusion | flops 1176305664 | bytes 4130816 | tf_op jit(solution)/shard_map/dot_general | solution.py:35
  288.0 0.0 copy-done.1
  (3 shorter events, 0.0 us)
Async XLA Ops:
  7.2 3.7 %copy-start = (bf16[512,1792]{1,0:T(8,128)(2,1)S(1)}, bf16[512,1792]{1,0:T(8,128)(2,1)}, u32[]{:S(2)}) copy-start(bf16[512,1792]{1,0:T(8,128)(2,1)} %param.8) | copy-start | bytes 5505028
  17.7 8.6 %copy-start.5 = (s32[512,1]{0,1:T(1,128)S(1)}, s32[512,1]{0,1:T(1,128)}, u32[]{:S(2)}) copy-start(s32[512,1]{0,1:T(1,128)} %param.11) | copy-start | bytes 6148
  17.7 46.0 %all-to-all-start = ((bf16[32,20,1792]{2,1,0:T(8,128)(2,1)}), bf16[32,20,1792]{2,1,0:T(8,128)(2,1)S(1)}, u32[]{:S(2)}, u32[]{:S(2)}) async-start(bf16[32,20,1792]{2,1,0:T(8,128)(2,1)} %reshape.132), calls=%async_computation | async-start | bytes 5505024 | tf_op jit(solution)/shard_map/all_to_all | solution.py:65
  63.8 42.3 %all-to-all-start.1 = ((bf16[32,20,1792]{2,1,0:T(8,128)(2,1)}), bf16[32,20,1792]{2,1,0:T(8,128)(2,1)}, u32[]{:S(2)}, u32[]{:S(2)}) async-start(bf16[32,20,1792]{2,1,0:T(8,128)(2,1)} %reshape.134), calls=%async_computation.1 | async-start | bytes 5505024 | tf_op jit(solution)/shard_map/all_to_all | solution.py:66
  68.6 88.5 %reduce-scatter.2.cloned.1.call-start = ((), (), s32[]{:S(2)}) async-start(), calls=%async_computation.4 | async-start | bytes 4915200 | tf_op jit(solution)/shard_map/reduce_scatter | solution.py:77
  70.7 6.5 %copy-start.2 = (bf16[640,1792]{1,0:T(8,128)(2,1)S(1)}, bf16[640,1792]{1,0:T(8,128)(2,1)}, u32[]{:S(2)}) copy-start(bf16[640,1792]{1,0:T(8,128)(2,1)} %reshape.133) | copy-start | bytes 6881284
  70.7 6.5 %copy-start.6 = (bf16[1,1792,1024]{2,1,0:T(8,128)(2,1)S(1)}, bf16[1,1792,1024]{2,1,0:T(8,128)(2,1)}, u32[]{:S(2)}) copy-start(bf16[1,1792,1024]{2,1,0:T(8,128)(2,1)} %param.12) | copy-start | bytes 11010052
  108.8 4.8 %copy-start.3 = (bf16[640,1,1024]{2,0,1:T(8,128)(2,1)S(1)}, bf16[640,1,1024]{2,0,1:T(8,128)(2,1)}, u32[]{:S(2)}) copy-start(bf16[640,1,1024]{2,0,1:T(8,128)(2,1)} %fusion.31) | copy-start | bytes 3932164
  108.8 4.8 %copy-start.4 = (bf16[640,1,1024]{2,0,1:T(8,128)(2,1)S(1)}, bf16[640,1,1024]{2,0,1:T(8,128)(2,1)}, u32[]{:S(2)}) copy-start(bf16[640,1,1024]{2,0,1:T(8,128)(2,1)} %fusion.34) | copy-start | bytes 3932164
  115.7 68.8 %all-gather.5.cloned.1.call-start = ((), (), s32[]{:S(2)}) async-start(), calls=%async_computation.6 | async-start | bytes 1638400 | tf_op jit(solution)/shard_map/all_gather | solution.py:95
  159.7 62.8 %all-gather.3.cloned.1.call-start = ((), (), s32[]{:S(2)}) async-start(), calls=%async_computation.5 | async-start | bytes 3276800 | tf_op jit(solution)/shard_map/all_gather | solution.py:87
  234.4 44.9 %all-to-all-start.2 = ((bf16[32,20,1792]{2,1,0:T(8,128)(2,1)}), bf16[32,20,1792]{2,1,0:T(8,128)(2,1)}, u32[]{:S(2)}, u32[]{:S(2)}) async-start(bf16[32,20,1792]{2,1,0:T(8,128)(2,1)} %reshape.136), calls=%async_computation.3 | async-start | bytes 5505024 | tf_op jit(solution)/shard_map/all_to_all | solution.py:102
  279.3 8.8 %copy-start.1 = (bf16[512,1792]{1,0:T(8,128)(2,1)S(1)}, bf16[512,1792]{1,0:T(8,128)(2,1)}, u32[]{:S(2)}) copy-start(bf16[512,1792]{1,0:T(8,128)(2,1)} %param.8) | copy-start | bytes 5505028
Sparse Core Ops, SparseCore 0:
  115.8 41.2 reduce-scatter.1
  159.8 24.6 all-gather.4
  186.7 35.7 all-gather.2
